TPU v7x, 32 devices: a whole 2x2x4 slice. The times are simulated.
32 devices in a mesh: px: 16 (over z, x, core), pz: 2 (over y).
Axes of the slice: x: 2, y: 2, z: 4, core: 2. Of those that a mesh axis runs over, the one named last changes fastest.
Arguments:
- base: float32 [3, 256, 256, 128], P(None, 'px', 'pz'), may hold values from -6 to 6
- adjoint: float32 [3, 256, 256, 128], P(None, 'px', 'pz'), may hold values from -6 to 6
- tangent: float32 [1, 3, 256, 256, 128], P(None, None, 'px', 'pz'), may hold values from -6 to 6
- second: float32 [1, 3, 256, 256, 128], P(None, None, 'px', 'pz'), may hold values from -6 to 6
- dealias_mask: int32 [256, 256], P('px', 'pz'), may hold values 0 or 1
- tau_rows: int32 [256, 256, 2], P('px', 'pz'), may hold values from 0 to 63
- tau_inverse: float32 [256, 256, 64, 128], P('px', 'pz'), may hold values from -1 to 2.5, as said below
Outputs:
- base_next: float32 [3, 256, 256, 128], P(None, 'px', 'pz')
- adjoint_next: float32 [3, 256, 256, 128], P(None, 'px', 'pz')
- tangent_next: float32 [1, 3, 256, 256, 128], P(None, None, 'px', 'pz')
- second_next: float32 [1, 3, 256, 256, 128], P(None, None, 'px', 'pz')
Inputs may be any that keep to these rules, and one draw needn't show every extreme that they name: `tau_inverse`: entry [kx, kz, a, p * 64 + b] maps the input at Chebyshev index 2 b + p to the output at index 2 a + p.
All inputs are finite; a program needn't handle non-finite values. No bound on the sum of `dealias_mask` on one device may be relied on, other than what follows from the above.
Results may differ from a plain program's by a relative error of at most 0.00013.
Values sent between devices are 32-bit elements; how exact they have to be, the bound alone decides.
A program may use at most 256 MiB of HBM per device.

v0:
```python
import math

import jax
import jax.numpy as jnp
from jax import lax
from jax.sharding import PartitionSpec as P

NX = 256
NZ = 256
NY = 128
DIRS = 1
HALF = 64


step_gain = 0.5


def hartley(length):
    indices = jnp.arange(length, dtype=jnp.int32)
    product = indices[:, None] * indices[None, :] % length
    angles = product.astype(jnp.float32) * (2.0 * math.pi / length)
    return (jnp.cos(angles) + jnp.sin(angles)) / math.sqrt(length)


def hartley_slope(length):
    indices = jnp.arange(length, dtype=jnp.int32)
    product = indices[:, None] * indices[None, :] % length
    angles = product.astype(jnp.float32) * (2.0 * math.pi / length)
    signed = jnp.where(indices < length // 2, indices, indices - length).astype(jnp.float32)
    return (
        (jnp.cos(angles) - jnp.sin(angles))
        * (signed * (2.0 * math.pi / length))[None, :]
        / math.sqrt(length)
    )


def chebyshev(length):
    indices = jnp.arange(length, dtype=jnp.int32)
    product = (2 * indices[:, None] + 1) * indices[None, :] % (4 * length)
    angles = product.astype(jnp.float32) * (math.pi / (2 * length))
    column_scale = jnp.where(indices == 0, math.sqrt(1.0 / length), math.sqrt(2.0 / length)).astype(
        jnp.float32
    )
    return jnp.cos(angles) * column_scale[None, :]


def chebyshev_slope(length):
    indices = jnp.arange(length, dtype=jnp.int32)
    product = (2 * indices[:, None] + 1) * indices[None, :] % (4 * length)
    angles = product.astype(jnp.float32) * (math.pi / (2 * length))
    nodes = jnp.sin((2 * indices + 1).astype(jnp.float32) * (math.pi / (2 * length)))
    column_scale = jnp.where(indices == 0, math.sqrt(1.0 / length), math.sqrt(2.0 / length)).astype(
        jnp.float32
    )
    column_scale = column_scale * indices.astype(jnp.float32)
    return jnp.sin(angles) * column_scale[None, :] / (length * nodes[:, None])


def crossed(first, other, axis):
    return jnp.roll(first, -1, axis) * jnp.roll(other, -2, axis) - jnp.roll(
        first, -2, axis
    ) * jnp.roll(other, -1, axis)


def forcings(velocity, vortex):
    grid_shape = velocity.shape[2:]
    base_v, adj_v = (velocity[0], velocity[1])
    tang_v, sec_v = (velocity[2 : 2 + DIRS], velocity[2 + DIRS :])
    base_o, adj_o = (vortex[0], vortex[1])
    tang_o, sec_o = (vortex[2 : 2 + DIRS], vortex[2 + DIRS :])
    force_base = crossed(base_v, base_o, 0)
    force_adjoint = crossed(base_v, adj_o, 0) + crossed(adj_v, base_o, 0)
    force_tangent = crossed(base_v[None], tang_o, 1) + crossed(tang_v, base_o[None], 1)
    force_second = (
        crossed(base_v[None], sec_o, 1)
        + crossed(sec_v, base_o[None], 1)
        + crossed(tang_v, adj_o[None], 1)
        + crossed(adj_v[None], tang_o, 1)
    )
    return jnp.concatenate(
        [
            force_base,
            force_adjoint,
            force_tangent.reshape((3 * DIRS,) + grid_shape),
            force_second.reshape((3 * DIRS,) + grid_shape),
        ],
        0,
    )


def placement_table(parity):
    outputs = jnp.arange(HALF, dtype=jnp.int32)[:, None]
    columns = jnp.arange(NY, dtype=jnp.int32)[None, :]
    return (columns == 2 * outputs + parity).astype(jnp.float32)


def body(base, adjoint, tangent, second, dealias_mask, tau_rows, tau_inverse):
    highest = lax.Precision.HIGHEST
    local_x = base.shape[1]
    local_z = base.shape[2]
    local_shape = (local_x, local_z, NY)
    count = 2 + 2 * DIRS
    hart_x = hartley(NX)
    hart_z = hartley(NZ)
    slope_xt = hartley_slope(NX)
    slope_zt = hartley_slope(NZ)
    cheb_y = chebyshev(NY)
    slope_yt = chebyshev_slope(NY)
    stacked = jnp.concatenate(
        [
            base,
            adjoint,
            tangent.reshape((3 * DIRS,) + local_shape),
            second.reshape((3 * DIRS,) + local_shape),
        ],
        0,
    )
    fields = stacked.shape[0]
    sideways = stacked.reshape((count, 3) + local_shape)[:, 0::2].reshape(
        (2 * count,) + local_shape
    )
    along_y = jnp.einsum("cxzn,jn->cxzj", stacked, cheb_y, precision=highest)
    slope_y = jnp.einsum("cxzn,jn->cxzj", sideways, slope_yt, precision=highest)
    groups_x = lax.axis_size("px")
    groups_z = lax.axis_size("pz")
    block_y = NY // groups_x
    block_x = NX // groups_z
    width = block_y * local_z

    def to_xlines(array):
        lead = array.shape[0]
        array = array.reshape((lead, local_x, local_z, groups_x, block_y))
        return array.transpose(0, 3, 1, 4, 2).reshape((lead, groups_x * local_x, width))

    whole_x, slope_whole = (
        lax.all_to_all(to_xlines(along_y), "px", split_axis=1, concat_axis=1, tiled=True),
        lax.all_to_all(to_xlines(slope_y), "px", split_axis=1, concat_axis=1, tiled=True),
    )
    values = jnp.einsum("ckm,xk->cxm", whole_x, hart_x, precision=highest)
    values = values.reshape((count, 3, NX, width))
    planar = whole_x.reshape((count, 3, NX, width))[:, 1:3].reshape((2 * count, NX, width))
    dx = jnp.einsum("ckm,xk->cxm", planar, slope_xt, precision=highest).reshape(
        (count, 2, NX, width)
    )
    dy = jnp.einsum("ckm,xk->cxm", slope_whole, hart_x, precision=highest).reshape(
        (count, 2, NX, width)
    )
    partial_value = jnp.stack(
        [values[:, 0], values[:, 1], values[:, 2], dy[:, 1], -dx[:, 1], dx[:, 0] - dy[:, 0]], 1
    )
    partial_value = partial_value.reshape((6 * count, NX, width))
    received = lax.all_to_all(partial_value, "pz", split_axis=1, concat_axis=1, tiled=True)
    received = received.reshape((6 * count, groups_z, block_x, block_y, local_z))
    received = received.transpose(0, 2, 3, 1, 4).reshape((count, 6, block_x, block_y, NZ))
    velocity = jnp.einsum("vcxjk,zk->vcxjz", received[:, 0:3], hart_z, precision=highest)
    rotated = jnp.einsum("vcxjk,zk->vcxjz", received[:, 3:6], hart_z, precision=highest)
    slope_v = jnp.einsum("vxjk,zk->vxjz", received[:, 1], slope_zt, precision=highest)
    slope_u = jnp.einsum("vxjk,zk->vxjz", received[:, 0], slope_zt, precision=highest)
    vortex = jnp.stack([rotated[:, 0] - slope_v, rotated[:, 1] + slope_u, rotated[:, 2]], 1)
    returned = jnp.einsum("cxjz,zk->cxjk", forcings(velocity, vortex), hart_z, precision=highest)
    returned = returned.reshape((fields, block_x, block_y, groups_z, local_z))
    returned = returned.transpose(0, 3, 1, 2, 4).reshape((fields, NX, width))
    mixed = lax.all_to_all(returned, "pz", split_axis=1, concat_axis=1, tiled=True)
    spectral_x = jnp.einsum("cxm,xk->ckm", mixed, hart_x, precision=highest)
    whole_y = lax.all_to_all(spectral_x, "px", split_axis=1, concat_axis=1, tiled=True)
    whole_y = whole_y.reshape((fields, groups_x, local_x, block_y, local_z))
    whole_y = whole_y.transpose(0, 2, 4, 1, 3).reshape((fields,) + local_shape)
    forcing_hat = jnp.einsum("cxzj,jn->cxzn", whole_y, cheb_y, precision=highest)
    right_side = (
        stacked + step_gain * forcing_hat * dealias_mask.astype(jnp.float32)[None, :, :, None]
    )
    positions = jnp.arange(HALF, dtype=jnp.int32)[None, None, :]
    even_side = right_side[..., 0::2]
    odd_side = right_side[..., 1::2]
    even_side = jnp.where(
        (positions != tau_rows[:, :, 0:1])[None], even_side, jnp.zeros_like(even_side)
    )
    odd_side = jnp.where(
        (positions != tau_rows[:, :, 1:2])[None], odd_side, jnp.zeros_like(odd_side)
    )
    even_solved = jnp.einsum(
        "xzab,cxzb->cxza", tau_inverse[..., :HALF], even_side, precision=highest
    )
    odd_solved = jnp.einsum("xzab,cxzb->cxza", tau_inverse[..., HALF:], odd_side, precision=highest)
    solved = jnp.einsum(
        "cxza,an->cxzn", even_solved, placement_table(0), precision=highest
    ) + jnp.einsum("cxza,an->cxzn", odd_solved, placement_table(1), precision=highest)
    base_next = solved[0:3]
    adjoint_next = solved[3:6]
    tangent_next = solved[6 : 6 + 3 * DIRS].reshape((DIRS, 3) + local_shape)
    second_next = solved[6 + 3 * DIRS :].reshape((DIRS, 3) + local_shape)
    return (base_next, adjoint_next, tangent_next, second_next)


def solution(mesh):
    in_specs = (
        P(None, "px", "pz", None),
        P(None, "px", "pz", None),
        P(None, None, "px", "pz", None),
        P(None, None, "px", "pz", None),
        P("px", "pz"),
        P("px", "pz", None),
        P("px", "pz", None, None),
    )
    out_specs = (
        P(None, "px", "pz", None),
        P(None, "px", "pz", None),
        P(None, None, "px", "pz", None),
        P(None, None, "px", "pz", None),
    )
    return jax.shard_map(body, mesh=mesh, in_specs=in_specs, out_specs=out_specs, check_vma=False)
```

profile of v0, /device:TPU:11, one launch (start us, length us, event | category | flops | bytes accessed | tf_op | source)
XLA Modules:
  0.0 2598.0 jit_solution(4196868939914721295)
XLA Ops:
  38.8 17.2 convolution_bitcast_fusion
  66.9 13.8 reshape.503
  80.8 17.9 copy.81
  98.6 122.4 %all-to-all-done.1 = f32[8,256,1024]{2,0,1:T(8,128)} async-done(((f32[8,256,1024]{2,0,1:T(8,128)}), f32[8,256,1024]{2,0,1:T(8,128)}, u32[]{:S(2)}, u32[]{:S(2)}) %all-to-all-start.1) | async-done | bytes 8388640 | tf_op jit(solution)/shard_map/all_to_all | solution.py:137
  226.4 19.2 fusion.33
  245.6 342.5 %all-to-all-done = f32[12,256,1024]{2,0,1:T(8,128)} async-done(((f32[12,256,1024]{2,0,1:T(8,128)}), f32[12,256,1024]{2,0,1:T(8,128)}, u32[]{:S(2)}, u32[]{:S(2)}) %all-to-all-start) | async-done | bytes 12582944 | tf_op jit(solution)/shard_map/all_to_all | solution.py:136
  588.2 17.5 copy.83
  605.7 19.6 fusion.79
  661.1 30.5 %copy.90 = f32[24,256,1024]{2,0,1:T(8,128)} copy(f32[24,256,1024]{2,1,0:T(8,128)S(1)} %bitcast.219) | data formatting | bytes 50331648 | tf_op jit(solution)/shard_map/reshape | solution.py:151
  691.6 279.3 %all_to_all.25 = f32[24,256,1024]{2,0,1:T(8,128)S(1)} all-to-all(f32[24,256,1024]{2,0,1:T(8,128)} %copy.90), channel_id=1, replica_groups=mesh['px'=16,'pz'=2] {'pz'}, dimensions={1} | all-to-all | bytes 50331648 | tf_op jit(solution)/shard_map/all_to_all | solution.py:152
  982.4 41.7 %copy.92 = f32[24,128,8,2,128]{4,3,1,2,0:T(2,128)} copy(f32[24,128,8,2,128]{4,2,0,1,3:T(8,128)} %bitcast.221) | data formatting | bytes 50331648 | tf_op jit(solution)/shard_map/transpose | solution.py:154
  1024.1 31.7 %reshape.514 = f32[4,6,128,8,256]{4,2,3,1,0:T(8,128)} reshape(f32[24,128,8,2,128]{4,3,1,2,0:T(2,128)} %copy.92) | data formatting | bytes 50331648 | tf_op jit(solution)/shard_map/reshape | solution.py:154
  1055.8 18.4 fusion.72
  1091.7 15.8 fusion.74
  1146.8 12.4 fusion.50
  1159.3 18.5 fusion.6
  1177.8 15.8 reshape.515
  1193.6 17.8 copy.179
  1211.4 14.0 reshape.516
  1225.4 17.9 copy.103
  1243.3 187.3 %all_to_all.26 = f32[12,256,1024]{2,0,1:T(8,128)S(1)} all-to-all(f32[12,256,1024]{2,0,1:T(8,128)} %copy.103), channel_id=1, replica_groups=mesh['px'=16,'pz'=2] {'pz'}, dimensions={1} | all-to-all | bytes 25165824 | tf_op jit(solution)/shard_map/all_to_all | solution.py:163
  1430.6 20.9 fusion.35
  1451.5 17.9 copy.105
  1478.0 360.5 %all-to-all-done.4 = f32[12,256,1024]{2,0,1:T(8,128)} async-done(((f32[12,256,1024]{2,0,1:T(8,128)}), f32[12,256,1024]{2,0,1:T(8,128)}, u32[]{:S(2)}, u32[]{:S(2)}) %all-to-all-start.4) | async-done | bytes 12582944 | tf_op jit(solution)/shard_map/all_to_all | solution.py:165
  1838.5 15.7 reshape.538
  1854.2 27.1 %multiply_add_fusion = f32[12,16,128,128]{3,2,1,0:T(8,128)} fusion(f32[16,128]{1,0:T(8,128)S(1)} %convert_multiply_fusion, f32[128]{0:T(128)S(1)} %copy-done.18, s32[128]{0:T(128)S(1)} %copy-done.20, f32[3,16,128,128]{3,2,1,0:T(8,128)S(1)} %bitcast.238, f32[3,16,128,128]{3,2,1,0:T(8,128)} %bitcast.241, f32[3,16,128,128]{3,2,1,0:T(8,128)} %param.8, ...), kind=kOutput, calls=%fused_computation.27 | convolution fusion | flops 4847812608 | bytes 37757952 | tf_op jit(solution)/shard_map/cxzj,jn->cxzn/dot_general | solution.py:168
  1881.3 216.2 %slice.416 = f32[12,16,128,64]{3,2,1,0:T(8,128)} slice(f32[12,16,128,128]{3,2,1,0:T(8,128)} %multiply_add_fusion), slice={[0:12:1], [0:16:1], [0:128:1], [1:128:2]} | slice | bytes 12582912 | tf_op jit(solution)/shard_map/slice | solution.py:174
  2097.5 213.2 %slice.413 = f32[12,16,128,64]{3,2,1,0:T(8,128)} slice(f32[12,16,128,128]{3,2,1,0:T(8,128)} %multiply_add_fusion), slice={[0:12:1], [0:16:1], [0:128:1], [0:128:2]} | slice | bytes 12582912 | tf_op jit(solution)/shard_map/slice | solution.py:173
  2322.5 111.6 %fusion.28 = f32[12,16,128,64]{3,0,2,1:T(8,128)} fusion(f32[16,128,64,128]{3,2,1,0:T(8,128)} %param.13, f32[12,16,128,64]{3,2,1,0:T(8,128)} %broadcast_select_fusion), kind=kOutput, calls=%fused_computation.41 | convolution fusion | flops 1207959552 | bytes 79691776 | tf_op jit(solution)/shard_map/xzab,cxzb->cxza/dot_general | solution.py:184
  2446.0 110.3 %fusion.23 = f32[12,16,128,64]{3,0,2,1:T(8,128)} fusion(f32[16,128,64,128]{3,2,1,0:T(8,128)} %param.13, f32[12,16,128,64]{3,2,1,0:T(8,128)} %broadcast_select_fusion.1), kind=kOutput, calls=%fused_computation.40 | convolution fusion | flops 1207959552 | bytes 79691776 | tf_op jit(solution)/shard_map/xzab,cxzb->cxza/dot_general | solution.py:181
  2556.4 12.5 fusion.17
  2568.9 18.7 fusion.38
  (93 shorter events, 200.7 us)
Async XLA Ops:
  31.6 7.2 copy-start.6
  31.6 189.5 %all-to-all-start.1 = ((f32[8,256,1024]{2,0,1:T(8,128)}), f32[8,256,1024]{2,0,1:T(8,128)}, u32[]{:S(2)}, u32[]{:S(2)}) async-start(f32[8,256,1024]{2,0,1:T(8,128)} %reshape.536), calls=%async_computation.1 | async-start | bytes 16777216 | tf_op jit(solution)/shard_map/all_to_all | solution.py:137
  38.7 17.3 copy-start.17
  38.8 17.3 copy-start.19
  221.1 367.1 %all-to-all-start = ((f32[12,256,1024]{2,0,1:T(8,128)}), f32[12,256,1024]{2,0,1:T(8,128)}, u32[]{:S(2)}, u32[]{:S(2)}) async-start(f32[12,256,1024]{2,0,1:T(8,128)} %copy.81), calls=%async_computation | async-start | bytes 33554432 | tf_op jit(solution)/shard_map/all_to_all | solution.py:136
  605.7 19.6 copy-start.2
  1055.8 18.4 copy-start
  1074.1 8.8 copy-start.3
  1107.5 9.6 copy-start.1
  1117.1 5.4 copy-start.4
  1122.5 3.3 copy-start.5
  1125.8 3.7 slice-start
  1129.5 2.9 copy-start.8
  1129.5 2.9 copy-start.9
  1132.4 2.1 copy-start.10
  1132.4 3.4 copy-start.11
  1135.8 5.8 copy-start.12
  1135.8 5.8 copy-start.13
  1469.4 7.2 copy-start.16
  1469.4 7.2 copy-start.15
  1469.4 369.1 %all-to-all-start.4 = ((f32[12,256,1024]{2,0,1:T(8,128)}), f32[12,256,1024]{2,0,1:T(8,128)}, u32[]{:S(2)}, u32[]{:S(2)}) async-start(f32[12,256,1024]{2,0,1:T(8,128)} %copy.105), calls=%async_computation.4 | async-start | bytes 33554432 | tf_op jit(solution)/shard_map/all_to_all | solution.py:165
  1478.0 376.2 %copy-start.7 = (f32[1,3,16,128,128]{4,3,2,1,0:T(8,128)S(1)}, f32[1,3,16,128,128]{4,3,2,1,0:T(8,128)}, u32[]{:S(2)}) copy-start(f32[1,3,16,128,128]{4,3,2,1,0:T(8,128)} %param.10) | copy-start | bytes 9437188
  1478.0 376.2 %copy-start.18 = (f32[128]{0:T(128)S(1)}, f32[128]{0:T(128)}, u32[]{:S(2)}) copy-start(f32[128]{0:T(128)} %copy-done.17) | copy-start | bytes 1540
  1478.0 376.2 %copy-start.20 = (s32[128]{0:T(128)S(1)}, s32[128]{0:T(128)}, u32[]{:S(2)}) copy-start(s32[128]{0:T(128)} %copy-done.19) | copy-start | bytes 1540
  2097.5 213.2 %copy-start.14 = (pred[16,128,64]{2,1,0:T(8,128)(4,1)S(1)}, pred[16,128,64]{2,1,0:T(8,128)(4,1)}, u32[]{:S(2)}) copy-start(pred[16,128,64]{2,1,0:T(8,128)(4,1)} %iota_compare_fusion) | copy-start | bytes 393220
  2434.1 122.2 %slice-start.1 = ((s8[16777216]{0:T(1024)(128)(4,1)}), s8[4194304]{0:T(1024)(128)(4,1)S(1)}, s32[]{:S(2)}) async-start(s8[16777216]{0:T(1024)(128)(4,1)} %bitcast.223), calls=%async_computation.6 | async-start | bytes 8388608
  2446.0 110.3 %slice-start.2 = ((s8[16777216]{0:T(1024)(128)(4,1)}), s8[4194304]{0:T(1024)(128)(4,1)S(1)}, s32[]{:S(2)}) async-start(s8[16777216]{0:T(1024)(128)(4,1)} %bitcast.223), calls=%async_computation.7 | async-start | bytes 8388608
  2446.0 110.3 %slice-start.3 = ((s8[16777216]{0:T(1024)(128)(4,1)}), s8[4194304]{0:T(1024)(128)(4,1)S(1)}, s32[]{:S(2)}) async-start(s8[16777216]{0:T(1024)(128)(4,1)} %bitcast.223), calls=%async_computation.8 | async-start | bytes 8388608
  2446.0 110.3 %slice-start.4 = ((s8[16777216]{0:T(1024)(128)(4,1)}), s8[4194304]{0:T(1024)(128)(4,1)S(1)}, s32[]{:S(2)}) async-start(s8[16777216]{0:T(1024)(128)(4,1)} %bitcast.223), calls=%async_computation.9 | async-start | bytes 8388608
where the time goes:
time: 2610 us; the launch traced here: 2600 us
  waiting for transfers between devices  825 us (32%)
  local copies, waits for them, and re-layouts  755 us (29%)
  blocking collectives  467 us (18%)
  matrix products  447 us (17%)
  other arithmetic  83.4 us (3%)
    all_to_all x1, waiting for transfers between devices, body(): lax.all_to_all(spectral_x, 'px', split_axis=1, concat_axis=1, tiled=True)  360 us
    all_to_all x1, waiting for transfers between devices, body(): lax.all_to_all(to_xlines(along_y), 'px', split_axis=1, concat_axis=1, til...  343 us
    all_to_all x1, blocking collectives, body(): lax.all_to_all(partial_value, 'pz', split_axis=1, concat_axis=1, tiled=True)  279 us
    slice x1, local copies, waits for them, and re-layouts, body(): odd_side = right_side[..., 1::2]  216 us
    slice x1, local copies, waits for them, and re-layouts, body(): even_side = right_side[..., 0::2]  213 us
    all_to_all x1, blocking collectives, body(): lax.all_to_all(returned, 'pz', split_axis=1, concat_axis=1, tiled=True)  187 us
    all_to_all x1, waiting for transfers between devices, body(): lax.all_to_all(to_xlines(slope_y), 'px', split_axis=1, concat_axis=1, til...  122 us
    dot_general x1, matrix products, body(): jnp.einsum('xzab,cxzb->cxza', tau_inverse[..., HALF:], odd_side, precisio...  112 us
  transfers between devices with their start and end apart: 3, of which 3 were waited for; matrix products, arithmetic and copies ran while one was open for 3% of the time, Pallas kernels for 0%

commit v1 on v0

v1 whole, which is shorter than its diff:
```python
import math

import jax
import jax.numpy as jnp
from jax import lax
from jax.sharding import PartitionSpec as P

NX = 256
NZ = 256
NY = 128
DIRS = 1
HALF = 64


step_gain = 0.5


def hartley(length):
    indices = jnp.arange(length, dtype=jnp.int32)
    product = indices[:, None] * indices[None, :] % length
    angles = product.astype(jnp.float32) * (2.0 * math.pi / length)
    return (jnp.cos(angles) + jnp.sin(angles)) / math.sqrt(length)


def hartley_slope(length):
    indices = jnp.arange(length, dtype=jnp.int32)
    product = indices[:, None] * indices[None, :] % length
    angles = product.astype(jnp.float32) * (2.0 * math.pi / length)
    signed = jnp.where(indices < length // 2, indices, indices - length).astype(jnp.float32)
    return (
        (jnp.cos(angles) - jnp.sin(angles))
        * (signed * (2.0 * math.pi / length))[None, :]
        / math.sqrt(length)
    )


def chebyshev(length):
    indices = jnp.arange(length, dtype=jnp.int32)
    product = (2 * indices[:, None] + 1) * indices[None, :] % (4 * length)
    angles = product.astype(jnp.float32) * (math.pi / (2 * length))
    column_scale = jnp.where(indices == 0, math.sqrt(1.0 / length), math.sqrt(2.0 / length)).astype(
        jnp.float32
    )
    return jnp.cos(angles) * column_scale[None, :]


def chebyshev_slope(length):
    indices = jnp.arange(length, dtype=jnp.int32)
    product = (2 * indices[:, None] + 1) * indices[None, :] % (4 * length)
    angles = product.astype(jnp.float32) * (math.pi / (2 * length))
    nodes = jnp.sin((2 * indices + 1).astype(jnp.float32) * (math.pi / (2 * length)))
    column_scale = jnp.where(indices == 0, math.sqrt(1.0 / length), math.sqrt(2.0 / length)).astype(
        jnp.float32
    )
    column_scale = column_scale * indices.astype(jnp.float32)
    return jnp.sin(angles) * column_scale[None, :] / (length * nodes[:, None])


def crossed(first, other, axis):
    return jnp.roll(first, -1, axis) * jnp.roll(other, -2, axis) - jnp.roll(
        first, -2, axis
    ) * jnp.roll(other, -1, axis)


def forcings(velocity, vortex):
    grid_shape = velocity.shape[2:]
    base_v, adj_v = (velocity[0], velocity[1])
    tang_v, sec_v = (velocity[2 : 2 + DIRS], velocity[2 + DIRS :])
    base_o, adj_o = (vortex[0], vortex[1])
    tang_o, sec_o = (vortex[2 : 2 + DIRS], vortex[2 + DIRS :])
    force_base = crossed(base_v, base_o, 0)
    force_adjoint = crossed(base_v, adj_o, 0) + crossed(adj_v, base_o, 0)
    force_tangent = crossed(base_v[None], tang_o, 1) + crossed(tang_v, base_o[None], 1)
    force_second = (
        crossed(base_v[None], sec_o, 1)
        + crossed(sec_v, base_o[None], 1)
        + crossed(tang_v, adj_o[None], 1)
        + crossed(adj_v[None], tang_o, 1)
    )
    return jnp.concatenate(
        [
            force_base,
            force_adjoint,
            force_tangent.reshape((3 * DIRS,) + grid_shape),
            force_second.reshape((3 * DIRS,) + grid_shape),
        ],
        0,
    )


def parity_order():
    columns = jnp.arange(NY, dtype=jnp.int32)
    return 2 * (columns % HALF) + columns // HALF


def parity_table():
    return (jnp.arange(NY, dtype=jnp.int32)[:, None] == parity_order()[None, :]).astype(jnp.float32)


def to_physical_pencil(along_y, slope_y, tables, local_x, local_z, precise):
    hart_x, hart_z, slope_xt, slope_zt = tables
    groups_x = lax.axis_size("px")
    groups_z = lax.axis_size("pz")
    count = along_y.shape[0] // 3
    block_y = NY // groups_x
    block_x = NX // groups_z
    width = block_y * local_z

    def to_xlines(array):
        lead = array.shape[0]
        array = array.reshape((lead, local_x, local_z, groups_x, block_y))
        return array.transpose(0, 3, 1, 4, 2).reshape((lead, groups_x * local_x, width))

    whole_x, slope_whole = (
        lax.all_to_all(to_xlines(along_y), "px", split_axis=1, concat_axis=1, tiled=True),
        lax.all_to_all(to_xlines(slope_y), "px", split_axis=1, concat_axis=1, tiled=True),
    )
    values = jnp.einsum("ckm,xk->cxm", whole_x, hart_x, precision=precise)
    values = values.reshape((count, 3, NX, width))
    planar = whole_x.reshape((count, 3, NX, width))[:, 1:3].reshape((2 * count, NX, width))
    dx = jnp.einsum("ckm,xk->cxm", planar, slope_xt, precision=precise).reshape(
        (count, 2, NX, width)
    )
    dy = jnp.einsum("ckm,xk->cxm", slope_whole, hart_x, precision=precise).reshape(
        (count, 2, NX, width)
    )
    partial_value = jnp.stack(
        [values[:, 0], values[:, 1], values[:, 2], dy[:, 1], -dx[:, 1], dx[:, 0] - dy[:, 0]], 1
    )
    partial_value = partial_value.reshape((6 * count, NX, width))
    received = lax.all_to_all(partial_value, "pz", split_axis=1, concat_axis=1, tiled=True)
    received = received.reshape((6 * count, groups_z, block_x, block_y, local_z))
    received = received.transpose(0, 2, 3, 1, 4).reshape((count, 6, block_x, block_y, NZ))
    velocity = jnp.einsum("vcxjk,zk->vcxjz", received[:, 0:3], hart_z, precision=precise)
    rotated = jnp.einsum("vcxjk,zk->vcxjz", received[:, 3:6], hart_z, precision=precise)
    slope_v = jnp.einsum("vxjk,zk->vxjz", received[:, 1], slope_zt, precision=precise)
    slope_u = jnp.einsum("vxjk,zk->vxjz", received[:, 0], slope_zt, precision=precise)
    vortex = jnp.stack([rotated[:, 0] - slope_v, rotated[:, 1] + slope_u, rotated[:, 2]], 1)
    force = forcings(velocity, vortex)
    fields = force.shape[0]
    returned = jnp.einsum("cxjz,zk->cxjk", force, hart_z, precision=precise)
    returned = returned.reshape((fields, block_x, block_y, groups_z, local_z))
    returned = returned.transpose(0, 3, 1, 2, 4).reshape((fields, NX, width))
    mixed = lax.all_to_all(returned, "pz", split_axis=1, concat_axis=1, tiled=True)
    spectral_x = jnp.einsum("cxm,xk->ckm", mixed, hart_x, precision=precise)
    whole_y = lax.all_to_all(spectral_x, "px", split_axis=1, concat_axis=1, tiled=True)
    whole_y = whole_y.reshape((fields, groups_x, local_x, block_y, local_z))
    return whole_y.transpose(1, 3, 0, 2, 4).reshape((NY, fields, local_x, local_z))


def through_slabs(lines, tables, local_x, local_z, precise):
    hart_x, hart_z, slope_xt, slope_zt = tables
    groups_x = lax.axis_size("px")
    groups_z = lax.axis_size("pz")
    block_y = NY // (groups_x * groups_z)
    lead = lines.shape[1]
    count = lead // 5
    moved = lax.all_to_all(lines, ("px", "pz"), split_axis=0, concat_axis=0, tiled=True)
    moved = moved.reshape((groups_x, groups_z, block_y, lead, local_x, local_z))
    moved = moved.transpose(2, 3, 0, 4, 1, 5).reshape((block_y, lead, NX, NZ))
    moved = moved.transpose(1, 0, 2, 3)
    planes = jnp.einsum("cjkz,xk->cjxz", moved, hart_x, precision=precise)
    planes = planes.reshape((5, count, block_y, NX, NZ))
    dx = jnp.einsum(
        "cjkz,xk->cjxz", moved[count : 3 * count], slope_xt, precision=precise
    ).reshape((2, count, block_y, NX, NZ))
    partial_vortex = jnp.stack([planes[4], -dx[1], dx[0] - planes[3]], 1)
    velocity = jnp.einsum("cvjxk,zk->vcjxz", planes[0:3], hart_z, precision=precise)
    rotated = jnp.einsum("vcjxk,zk->vcjxz", partial_vortex, hart_z, precision=precise)
    dz = jnp.einsum("cvjxk,zk->vcjxz", planes[0:2], slope_zt, precision=precise)
    vortex = jnp.stack(
        [rotated[:, 0] - dz[:, 1], rotated[:, 1] + dz[:, 0], rotated[:, 2]], 1
    )
    force = forcings(velocity, vortex)
    fields = force.shape[0]
    force = jnp.einsum("cjxz,zk->cjxk", force, hart_z, precision=precise)
    force = jnp.einsum("cjxz,xk->cjkz", force, hart_x, precision=precise)
    force = force.reshape((fields, block_y, groups_x, local_x, groups_z, local_z))
    force = force.transpose(2, 4, 1, 0, 3, 5).reshape((NY, fields, local_x, local_z))
    return lax.all_to_all(force, ("px", "pz"), split_axis=0, concat_axis=0, tiled=True)


def body(base, adjoint, tangent, second, dealias_mask, tau_rows, tau_inverse):
    precise = lax.Precision.HIGH
    local_x = base.shape[1]
    local_z = base.shape[2]
    local_shape = (local_x, local_z, NY)
    count = 2 + 2 * DIRS
    tables = (hartley(NX), hartley(NZ), hartley_slope(NX), hartley_slope(NZ))
    cheb_y = chebyshev(NY)
    slope_yt = chebyshev_slope(NY)
    stacked = jnp.concatenate(
        [
            base,
            adjoint,
            tangent.reshape((3 * DIRS,) + local_shape),
            second.reshape((3 * DIRS,) + local_shape),
        ],
        0,
    )
    fields = stacked.shape[0]
    by_velocity = stacked.reshape((count, 3) + local_shape)
    if NY % (lax.axis_size("px") * lax.axis_size("pz")) == 0:
        grouped = by_velocity.transpose(1, 0, 2, 3, 4).reshape(stacked.shape)
        along_y = jnp.einsum("cxzn,jn->jcxz", grouped, cheb_y, precision=precise)
        sideways = by_velocity.transpose(1, 0, 2, 3, 4)[0::2].reshape((2 * count,) + local_shape)
        slope_y = jnp.einsum("cxzn,jn->jcxz", sideways, slope_yt, precision=precise)
        lines = jnp.concatenate([along_y, slope_y], 1)
        whole_y = through_slabs(lines, tables, local_x, local_z, precise)
    else:
        sideways = by_velocity[:, 0::2].reshape((2 * count,) + local_shape)
        along_y = jnp.einsum("cxzn,jn->cxzj", stacked, cheb_y, precision=precise)
        slope_y = jnp.einsum("cxzn,jn->cxzj", sideways, slope_yt, precision=precise)
        whole_y = to_physical_pencil(along_y, slope_y, tables, local_x, local_z, precise)
    parity = parity_table()
    forcing_hat = jnp.einsum("jcxz,jq->cxzq", whole_y, chebyshev(NY)[:, parity_order()], precision=precise)
    sorted_side = jnp.einsum("cxzn,nq->cxzq", stacked, parity, precision=lax.Precision.HIGHEST)
    right_side = (
        sorted_side + step_gain * forcing_hat * dealias_mask.astype(jnp.float32)[None, :, :, None]
    )
    columns = jnp.arange(NY, dtype=jnp.int32)
    rows = jnp.where(columns < HALF, tau_rows[:, :, 0:1], tau_rows[:, :, 1:2])
    keep = rows != (columns % HALF)
    right_side = jnp.where(keep[None], right_side, 0.0)
    halves = (columns // HALF)[None, :] == jnp.arange(2, dtype=jnp.int32)[:, None]
    blocked = jnp.where(halves[None, :, None, None, :], right_side[:, None], 0.0)
    solved = jnp.einsum("xzaq,cpxzq->xzcpa", tau_inverse, blocked, precision=precise)
    places = parity.T.reshape((2, HALF, NY))
    solved = jnp.einsum(
        "xzca,an->cxzn", solved[:, :, :, 0], places[0], precision=lax.Precision.HIGHEST
    ) + jnp.einsum("xzca,an->cxzn", solved[:, :, :, 1], places[1], precision=lax.Precision.HIGHEST)
    base_next = solved[0:3]
    adjoint_next = solved[3:6]
    tangent_next = solved[6 : 6 + 3 * DIRS].reshape((DIRS, 3) + local_shape)
    second_next = solved[6 + 3 * DIRS :].reshape((DIRS, 3) + local_shape)
    return (base_next, adjoint_next, tangent_next, second_next)


def solution(mesh):
    in_specs = (
        P(None, "px", "pz", None),
        P(None, "px", "pz", None),
        P(None, None, "px", "pz", None),
        P(None, None, "px", "pz", None),
        P("px", "pz"),
        P("px", "pz", None),
        P("px", "pz", None, None),
    )
    out_specs = (
        P(None, "px", "pz", None),
        P(None, "px", "pz", None),
        P(None, None, "px", "pz", None),
        P(None, None, "px", "pz", None),
    )
    return jax.shard_map(body, mesh=mesh, in_specs=in_specs, out_specs=out_specs, check_vma=False)
```

time: 2610 us -> 1300 us (0.50)
  local copies, waits for them, and re-layouts: 755 us -> 223 us
  blocking collectives: 467 us -> 0 us
  matrix products: 447 us -> 253 us
  waiting for transfers between devices: 825 us -> 709 us
    all_to_all x2 -> x0, blocking collectives: 467 us -> none  [the longest x1 279 us: body(): lax.all_to_all(partial_value, 'pz', split_axis=1, concat_axis=1, tiled=True)]
    slice x7 -> x5, local copies, waits for them, and re-layouts: 433 us -> 30.8 us  [the longest x2 12.7 us: body(): by_velocity.transpose(1, 0, 2, 3, 4)[0::2]]
    dot_general x16 -> x14, matrix products: 447 us -> 253 us  [the longest x1 59.3 us: body(): jnp.einsum('xzaq,cpxzq->xzcpa', tau_inverse, blocked, precision=precise)]
    all_to_all x3 -> x2, waiting for transfers between devices: 825 us -> 709 us  [the longest x1 451 us: through_slabs(): lax.all_to_all(lines, ('px', 'pz'), split_axis=0, concat_axis=0, tiled=True)]
    reshape x12 -> x4, local copies, waits for them, and re-layouts: 201 us -> 88.7 us  [the longest x1 35.3 us: through_slabs(): moved = moved.reshape((groups_x, groups_z, block_y, lead, local_x, local_z))]
    transpose x2 -> x1, local copies, waits for them, and re-layouts: 59.5 us -> 11.3 us  [body(): grouped = by_velocity.transpose(1, 0, 2, 3, 4).reshape(stacked.shape)]
  transfers between devices with their start and end apart: 3 -> 2, of which waited for: 3 -> 2; matrix products, arithmetic and copies ran while one was open for 3% -> 1% of each run, Pallas kernels for 0% -> 0%
where the time goes in v1:
time: 1300 us; the launch traced here: 1280 us
  waiting for transfers between devices  709 us (55%)
  matrix products  253 us (19%)
  local copies, waits for them, and re-layouts  223 us (17%)
  other arithmetic  62.6 us (5%)
  starting transfers between devices  29.1 us (2%)
    all_to_all x1, waiting for transfers between devices, through_slabs(): lax.all_to_all(lines, ('px', 'pz'), split_axis=0, concat_axis=0, tiled=True)  451 us
    all_to_all x1, waiting for transfers between devices, through_slabs(): lax.all_to_all(force, ('px', 'pz'), split_axis=0, concat_axis=0, tiled=True)  258 us
    dot_general x1, matrix products, body(): jnp.einsum('xzaq,cpxzq->xzcpa', tau_inverse, blocked, precision=precise)  59.3 us
    reshape x1, local copies, waits for them, and re-layouts, through_slabs(): moved = moved.reshape((groups_x, groups_z, block_y, lead, local_x, local_z))  35.3 us
    reshape x2, local copies, waits for them, and re-layouts, through_slabs(): force.reshape((fields, block_y, groups_x, local_x, groups_z, local_z))  26.8 us
    reshape x1, local copies, waits for them, and re-layouts, through_slabs(): moved = moved.transpose(2, 3, 0, 4, 1, 5).reshape((block_y, lead, NX, NZ))  26.6 us
    dot_general x1, matrix products, body(): jnp.einsum('jcxz,jq->cxzq', whole_y, chebyshev(NY)[:, parity_order()], pr...  26.4 us
  transfers between devices with their start and end apart: 2, of which 2 were waited for; matrix products, arithmetic and copies ran while one was open for 1% of the time, Pallas kernels for 0%

profile of v1, /device:TPU:11, one launch (start us, length us, event | category | flops | bytes accessed | tf_op | source)
XLA Modules:
  0.0 1277.2 jit_solution(7592314410872680082)
XLA Ops:
  14.3 11.3 copy.133
  25.6 8.9 copy.134
  35.6 9.3 fusion.76
  57.7 14.3 %copy.136 = f32[128,20,16,128]{3,2,1,0:T(8,128)} copy(f32[128,20,16,128]{3,0,2,1:T(8,128)S(1)} %pad_maximum_fusion) | data formatting | bytes 41943040 | tf_op jit(solution)/shard_map/concatenate | solution.py:208
  72.0 7.0 all-to-all-start
  79.0 450.8 %all-to-all-done = f32[128,20,16,128]{3,2,1,0:T(8,128)} async-done(((f32[128,20,16,128]{3,2,1,0:T(8,128)}), f32[128,20,16,128]{3,2,1,0:T(8,128)}, u32[]{:S(2)}, u32[]{:S(2)}) %all-to-all-start) | async-done | bytes 20971552 | tf_op jit(solution)/shard_map/all_to_all | solution.py:158
  529.8 35.3 %copy.236 = f32[16,2,4,20,16,128]{5,1,4,0,2,3:T(2,128)} copy(f32[16,2,4,20,16,128]{5,4,3,2,1,0:T(8,128)} %bitcast.20) | data formatting | bytes 41943040 | tf_op jit(solution)/shard_map/reshape | solution.py:159
  565.1 26.6 %reshape.506 = f32[4,20,256,256]{3,2,0,1:T(8,128)} reshape(f32[4,20,16,16,2,128]{5,4,3,2,0,1:T(2,128)} %bitcast.213) | data formatting | bytes 41943040 | tf_op jit(solution)/shard_map/reshape | solution.py:160
  591.7 20.7 %convolution_bitcast_fusion = f32[20,4,256,256]{3,2,1,0:T(8,128)} fusion(f32[4,20,256,256]{3,2,0,1:T(8,128)} %reshape.506), kind=kOutput, calls=%fused_computation.43 | convolution fusion | flops 8054112256 | bytes 41943040 | tf_op jit(solution)/shard_map/cjkz,xk->cjxz/dot_general | solution.py:162
  612.4 7.6 slice.445
  620.1 10.5 slice.435
  630.6 16.4 %convolution_bitcast_fusion.2 = f32[4,3,4,256,256]{3,4,2,0,1:T(8,128)S(1)} fusion(f32[3,4,4,256,256]{4,3,2,1,0:T(8,128)} %bitcast.216), kind=kOutput, calls=%fused_computation.49 | convolution fusion | flops 4832886784 | bytes 25165824 | tf_op jit(solution)/shard_map/cvjxk,zk->vcjxz/dot_general | solution.py:168
  655.4 11.8 fusion.35
  667.2 11.0 slice_bitcast_fusion.2
  678.2 14.7 %fusion.32 = f32[4,2,4,256,256]{3,4,2,1,0:T(8,128)} fusion(f32[2,4,4,256,256]{4,3,2,1,0:T(8,128)} %bitcast.218, f32[256]{0:T(256)S(1)} %fusion.94), kind=kOutput, calls=%fused_computation.57 | convolution fusion | flops 3222339584 | bytes 16778240 | tf_op jit(solution)/shard_map/cvjxk,zk->vcjxz/dot_general | solution.py:170
  692.9 10.1 fusion.20
  712.8 8.4 fusion.52
  733.8 12.0 fusion.41
  745.8 17.4 %fusion.6 = f32[12,4,256,256]{3,2,1,0:T(8,128)} fusion(f32[3,4,256,256]{2,3,1,0:T(8,128)} %fusion.41, f32[3,4,256,256]{2,3,1,0:T(8,128)} %subtract_add_fusion, f32[3,4,256,256]{2,3,1,0:T(8,128)} %subtract_add_fusion.1, f32[3,4,256,256]{2,3,1,0:T(8,128)} %multiply_subtract_fusion), kind=kOutput, calls=%fused_computation.13 | convolution fusion | flops 4842323968 | bytes 25165824 | tf_op jit(solution)/shard_map/cjxz,zk->cjxk/dot_general | solution.py:176
  763.1 17.7 %convolution_bitcast_fusion.1 = f32[12,4,256,256]{3,2,1,0:T(8,128)} fusion(f32[12,4,256,256]{3,2,1,0:T(8,128)} %fusion.6), kind=kOutput, calls=%fused_computation.48 | convolution fusion | flops 4832886784 | bytes 25165824 | tf_op jit(solution)/shard_map/cjxz,xk->cjkz/dot_general | solution.py:177
  780.8 15.9 %reshape.507 = f32[12,4,16,16,2,128]{5,4,3,2,1,0:T(2,128)} reshape(f32[12,4,256,256]{3,2,1,0:T(8,128)} %convolution_bitcast_fusion.1) | data formatting | bytes 25165824 | tf_op jit(solution)/shard_map/reshape | solution.py:178
  796.7 10.9 copy.169
  807.6 22.1 %all-to-all-start.1 = ((f32[128,12,16,128]{3,2,1,0:T(8,128)}), f32[128,12,16,128]{3,2,1,0:T(8,128)}, u32[]{:S(2)}, u32[]{:S(2)}) async-start(f32[128,12,16,128]{3,2,1,0:T(8,128)} %bitcast.214), calls=%async_computation.1 | async-start | bytes 25165824 | tf_op jit(solution)/shard_map/all_to_all | solution.py:180
  831.6 11.0 fusion.87
  842.6 257.8 %all-to-all-done.1 = f32[128,12,16,128]{3,2,1,0:T(8,128)} async-done(((f32[128,12,16,128]{3,2,1,0:T(8,128)}), f32[128,12,16,128]{3,2,1,0:T(8,128)}, u32[]{:S(2)}, u32[]{:S(2)}) %all-to-all-start.1) | async-done | bytes 12582944 | tf_op jit(solution)/shard_map/all_to_all | solution.py:180
  1100.4 26.4 %add_select_fusion = f32[12,16,128,128]{3,2,1,0:T(8,128)} fusion(f32[12,16,128,128]{3,2,1,0:T(8,128)} %fusion.87, f32[16,128]{1,0:T(8,128)S(1)} %convert_multiply_fusion, pred[16,128,128]{2,1,0:T(8,128)(4,1)S(1)} %select_compare_fusion, f32[128,12,16,128]{3,2,1,0:T(8,128)} %all-to-all-done.1, f32[128,128]{1,0:T(8,128)S(1)} %gather_fusion), kind=kOutput, calls=%fused_computation.30 | convolution fusion | flops 2425356288 | bytes 38084608 | tf_op jit(solution)/shard_map/jcxz,jq->cxzq/dot_general | solution.py:216
  1126.8 19.5 %copy.171 = f32[12,16,128,128]{3,0,2,1:T(8,128)} copy(f32[12,16,128,128]{3,2,1,0:T(8,128)} %add_select_fusion) | data formatting | bytes 25165824 | tf_op jit(solution)/shard_map/jit(_where)/select_n | solution.py:224
  1146.3 59.3 %fusion = f32[16,128,12,2,64]{4,2,3,1,0:T(8,128)} fusion(f32[16,128,64,128]{3,2,1,0:T(8,128)} %param.13, f32[12,16,128,128]{3,0,2,1:T(8,128)} %copy.171, pred[2,128]{1,0:T(4,128)(4,1)S(1)} %iota_compare_fusion.2), kind=kOutput, calls=%fused_computation.1 | convolution fusion | flops 2422210560 | bytes 92274944 | tf_op jit(solution)/shard_map/xzaq,cpxzq->xzcpa/dot_general | solution.py:227
  1205.6 17.8 %slice_bitcast_fusion.1 = (f32[16,128,12,64]{3,2,1,0:T(8,128)}, f32[16,128,12,64]{3,2,1,0:T(8,128)S(1)}) fusion(f32[16,128,12,2,64]{4,2,3,1,0:T(8,128)} %fusion), kind=kLoop, calls=%fused_computation.7 | loop fusion | bytes 25165824 | tf_op jit(solution)/shard_map/squeeze | solution.py:230
  1223.5 11.4 fusion.14
  1234.9 20.4 %add_bitcast_fusion = f32[12,16,128,128]{2,3,0,1:T(8,128)} fusion(f32[128,16,128,12]{2,0,3,1:T(8,128)} %fusion.14, f32[16,128,12,64]{3,2,1,0:T(8,128)} %get-tuple-element.20, pred[128,128]{1,0:T(32,128)(4,1)S(1)} %iota_compare_fusion.1), kind=kOutput, calls=%fused_computation.29 | convolution fusion | flops 2419064832 | bytes 31465472 | tf_op jit(solution)/shard_map/xzca,an->cxzn/dot_general | solution.py:229
  1255.2 8.9 slice_bitcast_fusion.3
  (65 shorter events, 73.1 us)
Async XLA Ops:
  0.6 44.3 %copy-start.12 = (s32[128]{0:T(128)}, s32[128]{0:T(128)S(1)}, u32[]{:S(2)}) copy-start(s32[128]{0:T(128)S(1)} %multiply_add_fusion) | copy-start | bytes 1540
  6.0 4.5 copy-start
  25.6 8.9 copy-start.14
  25.6 10.0 copy-start.2
  72.0 457.8 %all-to-all-start = ((f32[128,20,16,128]{3,2,1,0:T(8,128)}), f32[128,20,16,128]{3,2,1,0:T(8,128)}, u32[]{:S(2)}, u32[]{:S(2)}) async-start(f32[128,20,16,128]{3,2,1,0:T(8,128)} %copy.136), calls=%async_computation | async-start | bytes 41943040 | tf_op jit(solution)/shard_map/all_to_all | solution.py:158
  678.2 14.7 %copy-start.6 = (f32[4,1,4,256,256]{4,3,2,0,1:T(8,128)S(1)}, f32[4,1,4,256,256]{4,3,2,0,1:T(8,128)}, u32[]{:S(2)}) copy-start(f32[4,1,4,256,256]{4,3,2,0,1:T(8,128)} %get-tuple-element.24) | copy-start | bytes 12582916
  712.8 8.4 copy-start.1
  712.8 8.4 copy-start.3
  721.2 2.3 copy-start.5
  723.5 5.5 copy-start.4
  723.5 5.5 copy-start.8
  723.5 5.5 copy-start.9
  807.6 22.1 %copy-start.13 = (s32[128]{0:T(128)S(1)}, s32[128]{0:T(128)}, u32[]{:S(2)}) copy-start(s32[128]{0:T(128)} %copy-done.12) | copy-start | bytes 1540
  807.6 22.1 %copy-start.15 = (f32[128]{0:T(128)S(1)}, f32[128]{0:T(128)}, u32[]{:S(2)}) copy-start(f32[128]{0:T(128)} %copy-done.14) | copy-start | bytes 1540
  807.6 23.1 %copy-start.11 = (s32[16,128]{1,0:T(8,128)S(1)}, s32[16,128]{1,0:T(8,128)}, u32[]{:S(2)}) copy-start(s32[16,128]{1,0:T(8,128)} %param.11) | copy-start | bytes 24580
  807.6 23.2 %copy-start.10 = (s32[16,128,2]{1,2,0:T(2,128)S(1)}, s32[16,128,2]{1,2,0:T(2,128)}, u32[]{:S(2)}) copy-start(s32[16,128,2]{1,2,0:T(2,128)} %param.12) | copy-start | bytes 49156
  807.6 24.0 %copy-start.7 = (f32[1,3,16,128,128]{4,3,2,1,0:T(8,128)S(1)}, f32[1,3,16,128,128]{4,3,2,1,0:T(8,128)}, u32[]{:S(2)}) copy-start(f32[1,3,16,128,128]{4,3,2,1,0:T(8,128)} %param.10) | copy-start | bytes 9437188
  807.6 292.7 %all-to-all-start.1 = ((f32[128,12,16,128]{3,2,1,0:T(8,128)}), f32[128,12,16,128]{3,2,1,0:T(8,128)}, u32[]{:S(2)}, u32[]{:S(2)}) async-start(f32[128,12,16,128]{3,2,1,0:T(8,128)} %bitcast.214), calls=%async_computation.1 | async-start | bytes 25165824 | tf_op jit(solution)/shard_map/all_to_all | solution.py:180
